TPU v7x, 32 devices: a whole 2x2x4 slice. The times are simulated.
32 devices in a mesh: blk: 16 (over z, y, core), rep: 2 (over x).
Axes of the slice: x: 2, y: 2, z: 4, core: 2. Of those that a mesh axis runs over, the one named last changes fastest.
Arguments:
- features: bfloat16 [32768, 256], P(('blk', 'rep')), may hold values from -6 to 6
- aggregated: bfloat16 [32768, 256], P(('blk', 'rep')), may hold values from -6 to 6
- out_grad: bfloat16 [32768, 256], P(('blk', 'rep')), may hold values from -6 to 6
- w_self: bfloat16 [256, 256], replicated, may hold values from -0.375 to 0.375
- w_neigh: bfloat16 [256, 256], replicated, may hold values from -0.375 to 0.375
- tiles: bfloat16 [16, 16, 8, 128, 128], P('blk'), may hold values from -0.0625 to 0.0625
- tile_rows: int32 [16, 16, 8], P('blk'), may hold values from 0 to 15
- tile_cols: int32 [16, 16, 8], P('blk'), may hold values from 0 to 15
- tile_counts: int32 [16, 16], P('blk'), may hold values from 0 to 8, as said below
Outputs:
- feature_grad: float32 [32768, 256], P(('blk', 'rep'))
- self_grad: float32 [256, 256], replicated
- neigh_grad: float32 [256, 256], replicated
Inputs may be any that keep to these rules, and one draw needn't show every extreme that they name: `tile_counts`: at most 8; some pair of blocks uses all 8 slots; tiles, rows and columns of slots beyond the count carry no meaning.
All inputs are finite; a program needn't handle non-finite values.
Results may differ from a plain program's by a relative error of at most 0.00082.
Values may be sent and summed in bfloat16 or wider, within the bound.
A program may use at most 64 MiB of HBM per device.

v0:
```python
import functools

import jax
import jax.numpy as jnp
from jax import lax
from jax.experimental import pallas as pl
from jax.experimental.pallas import tpu as pltpu
from jax.sharding import PartitionSpec as P

MESH = pl.DeviceIdType.MESH
CORES, ROWS_Y = 2, 2


PIECES = 2


def positions(line):
    last = 2 * (line - 1) + 1
    own = lambda d, w: 2 * (d - 1) + 1 + w if d else w
    ends = {}
    for d in range(line):
        ends[d, 0, 0] = own(d, 1) + 0.5
        ends[d, 1, 0] = 2.5 if d == 0 else min(own(d, 1) + 3, last + (d == line - 1) * 0.8) + 0.1
    for d in range(line):
        for other in range(2):
            ends[d, other, 1] = ends[d, other, 0] + (0.1 if ends[d, other, 0] > last else 0.95)
    return ends


def layer_kernel(
    blocks,
    copies,
    scale,
    rows_ref,
    cols_ref,
    counts_ref,
    features_ref,
    aggregated_ref,
    grad_ref,
    w_self_ref,
    w_neigh_ref,
    tiles_ref,
    base_ref,
    got_ref,
    sum_ref,
    rows_v,
    counts_v,
    rows_s,
    cols_s,
    counts_s,
    features_v,
    aggregated_v,
    grad_v,
    w_self_v,
    w_neigh_v,
    tiles_v,
    g,
    across,
    current,
    chain,
    links_v,
    links_s,
    base_v,
    back,
    terms,
    from_core,
    half_sum,
    from_x,
    quarter_sum,
    from_plane,
    total,
    local_sem,
    send_sem,
    recv_sem,
    x_send,
    back_send,
    back_recv,
    core_send,
    core_recv,
    pair_send,
    pair_recv,
    plane_send,
    plane_recv,
):
    b = lax.axis_index("blk")
    r = lax.axis_index("rep")
    plane = CORES * ROWS_Y
    line = blocks // plane
    z, y, c = b // plane, (b // CORES) % ROWS_Y, b % CORES
    near_x = (b, 1 - r)
    near_core = (z * plane + y * CORES + (1 - c), r)
    near_y = (z * plane + (1 - y) * CORES + c, r)
    up, down = (b + plane, r), (b - plane, r)
    has_up, has_down = z < line - 1, z > 0
    never = z < 0
    always = z >= 0
    pieces, piece_rows, width = g.shape[2:]
    slots, side = tiles_v.shape[1], tiles_v.shape[2]
    share_tiles = pieces * piece_rows // side
    seats = line * ROWS_Y
    seat = z * ROWS_Y + y
    end_of = lambda zz: (zz == 0) | (zz == line - 1)

    def local(src, dst, n):
        return pltpu.make_async_copy(src, dst, local_sem.at[n])

    loads = [
        local(grad_ref, grad_v, 0),
        local(w_neigh_ref, w_neigh_v, 1),
        local(features_ref, features_v, 2),
        local(aggregated_ref, aggregated_v, 3),
        local(rows_ref, rows_v, 4),
        local(counts_ref, counts_v, 5),
        local(rows_ref, rows_s, 6),
        local(cols_ref, cols_s, 7),
        local(counts_ref, counts_s, 8),
        local(w_self_ref, w_self_v, 9),
        local(tiles_ref, tiles_v, 10),
    ]
    for load in loads:
        load.start()

    barrier = pltpu.get_barrier_semaphore()

    def greet(device):
        pl.semaphore_signal(barrier, inc=1, device_id=device, device_id_type=MESH)

    def seat_device(step):
        other = (seat + step) % seats
        return other, ((other // ROWS_Y) * plane + (other % ROWS_Y) * CORES + c, r)

    greet(near_x)
    greet(near_core)

    @pl.loop(1, seats)
    def _(step):
        greet(seat_device(step)[1])

    loads[0].wait()
    loads[1].wait()

    def message(which, h):
        return lax.dot_general(
            grad_v[pl.ds(h * piece_rows, piece_rows), :],
            w_neigh_v[pl.ds(pl.multiple_of(which * width, width), width), :],
            (((1,), (1,)), ((), ())),
            preferred_element_type=jnp.float32,
        ).astype(g.dtype)

    for h in range(pieces):
        g[b, r, h] = message(r, h)
    for h in range(pieces):
        across[h] = message(1 - r, h)

    pl.semaphore_wait(barrier, 2 + seats - 1)

    def send(block, share, h, way, device):
        return pltpu.make_async_remote_copy(
            src_ref=g.at[block, share, h],
            dst_ref=g.at[block, share, h],
            send_sem=send_sem.at[way, block, share, h],
            recv_sem=recv_sem.at[block, share, h],
            device_id=device,
            device_id_type=MESH,
        )

    def x_copy(h):
        return pltpu.make_async_remote_copy(
            src_ref=across.at[h],
            dst_ref=g.at[b, r, h],
            send_sem=x_send.at[h],
            recv_sem=recv_sem.at[b, r, h],
            device_id=near_x,
            device_id_type=MESH,
        )

    def arrived(block, share, h):
        send(block, share, h, 3, near_core).wait_recv()

    def pass_on(block, share, h, go_up, go_down, go_y):
        @pl.when(go_up)
        def _():
            send(block, share, h, 0, up).start()

        @pl.when(go_down)
        def _():
            send(block, share, h, 1, down).start()

        @pl.when(go_y)
        def _():
            send(block, share, h, 2, near_y).start()

        send(block, share, h, 3, near_core).start()

    def share_of(which):
        return r if which == 0 else 1 - r

    def there(zz):
        return (zz >= 0) & (zz < line)

    def own_line(d, which):
        share = share_of(which)

        @pl.loop(0, pieces)
        def _(h):
            for sign in (-1, 1):
                zz = z + sign * d

                @pl.when(there(zz))
                def _():
                    block = zz * plane + y * CORES + c
                    arrived(block, share, h)
                    pass_on(
                        block,
                        share,
                        h,
                        has_up if sign < 0 else never,
                        has_down if sign > 0 else never,
                        jnp.logical_not(end_of(zz)) if which else always,
                    )

    def from_across():
        @pl.loop(0, pieces)
        def _(h):
            arrived(b, 1 - r, h)
            pass_on(b, 1 - r, h, has_up, has_down, always)

    def from_y(d, which):
        share = share_of(which)

        @pl.loop(0, pieces)
        def _(h):
            for sign in (-1, 1) if d else (0,):
                zz = z + sign * d
                wanted = there(zz)
                if which and d:
                    wanted = wanted & jnp.logical_not(end_of(zz))

                @pl.when(wanted)
                def _():
                    block = zz * plane + (1 - y) * CORES + c
                    arrived(block, share, h)
                    onward = which == 1 and d == 0
                    pass_on(
                        block,
                        share,
                        h,
                        has_up & (z == 0) if onward else never,
                        has_down & (z == line - 1) if onward else never,
                        never,
                    )

    def end_line(d):
        share = share_of(1)

        @pl.loop(0, pieces)
        def _(h):
            for sign in (-1, 1):
                zz = z + sign * d

                @pl.when(there(zz) & end_of(zz))
                def _():
                    block = zz * plane + (1 - y) * CORES + c
                    arrived(block, share, h)
                    pass_on(
                        block,
                        share,
                        h,
                        has_up if sign < 0 else never,
                        has_down if sign > 0 else never,
                        never,
                    )

    ends = positions(line)
    order = sorted(ends, key=lambda group: (ends[group], group))
    starts, count = {}, 0
    for group in order:
        starts[group] = count
        count += 2 if group[0] else 1
    nothing = count * slots

    def block_of(zz, other_y, other_core):
        yy = 1 - y if other_y else y
        cc = 1 - c if other_core else c
        return zz * plane + yy * CORES + cc

    def chain_links():
        for n in (4, 5, 6, 7, 8):
            loads[n].wait()
        slot = lax.broadcasted_iota(jnp.int32, rows_v.shape, 0)
        lane = lax.broadcasted_iota(jnp.int32, rows_v.shape, 1)
        wanted = jnp.where(slot < counts_v[...], rows_v[...], -2)
        candidates = [
            (starts[group] + i, group, sign)
            for group in order
            for i, sign in enumerate((-1, 1) if group[0] else (0,))
        ]
        own = slot
        found = []
        for index, (d, other_y, other_core), sign in candidates:
            zz = z + sign * d
            ok = there(zz)
            block = jnp.where(ok, block_of(zz, other_y, other_core), 0)
            own = jnp.where((lane == block) & ok, slot + index * slots, own)
            found.append((index * slots, block, ok))

        def step(k, carry):
            before, last = carry
            for first, block, ok in found:
                ok = ok & (k < counts_s[0, block])
                row = jnp.where(ok, rows_s[k, block], -1)
                key = first + k
                before = jnp.where((wanted == row) & (own > key), jnp.maximum(before, key), before)
                last = jnp.where(lane == row, jnp.maximum(last, key), last)
            return before, last

        none = jnp.full(rows_v.shape, -1, jnp.int32)
        before, last = lax.fori_loop(0, slots, step, (none, none))
        links_v[0] = jnp.where(before < 0, nothing, before)
        links_v[1] = jnp.where(last < 0, nothing, last)
        chain[nothing] = jnp.zeros(chain.shape[1:], chain.dtype)

    def links_copy():
        return local(links_v, links_s, 11)

    def multiply(group):
        d, other_y, other_core = group
        first = starts[group]

        def one(i):
            zz = z + (2 * i - 1) * d

            @pl.when(there(zz))
            def _():
                block = block_of(zz, other_y, other_core)
                if other_core:

                    @pl.loop(0, pieces)
                    def _(h):
                        for share in range(copies):
                            arrived(block, share, h)

                seat_of = first + i
                current[seat_of] = g[block].reshape(current.shape[1:])
                products = []
                for k in range(slots):
                    products.append(
                        jnp.dot(
                            tiles_v[block, k],
                            current[seat_of, cols_s[k, block]],
                            preferred_element_type=jnp.float32,
                        )
                    )
                for k in range(slots):
                    chain[seat_of * slots + k] = products[k] + chain[links_s[0, k, block]]

        if d:

            @pl.loop(0, 2)
            def _(i):
                one(i)
        else:
            one(0)

    out_width = total.shape[1]
    half, quarter = total.shape[0] // 2, total.shape[0] // 4
    part = quarter // seats

    def core_copy():
        return pltpu.make_async_remote_copy(
            src_ref=terms.at[pl.ds((1 - c) * half, half)],
            dst_ref=from_core,
            send_sem=core_send.at[0],
            recv_sem=core_recv.at[0],
            device_id=near_core,
            device_id_type=MESH,
        )

    def pair_copy():
        return pltpu.make_async_remote_copy(
            src_ref=half_sum.at[pl.ds((1 - r) * quarter, quarter)],
            dst_ref=from_x,
            send_sem=pair_send.at[0],
            recv_sem=pair_recv.at[0],
            device_id=near_x,
            device_id_type=MESH,
        )

    def part_copy(step, slot):
        other, device = seat_device(step)
        return pltpu.make_async_remote_copy(
            src_ref=quarter_sum.at[pl.ds(other * part, part)],
            dst_ref=from_plane.at[slot],
            send_sem=plane_send.at[0, other],
            recv_sem=plane_recv.at[0, slot],
            device_id=device,
            device_id_type=MESH,
        )

    def share_copy(step, owner):
        other, device = seat_device(step)
        where = pl.ds(c * half + r * quarter + owner * part, part)
        return pltpu.make_async_remote_copy(
            src_ref=total.at[where],
            dst_ref=total.at[where],
            send_sem=plane_send.at[1, other],
            recv_sem=plane_recv.at[1, owner],
            device_id=device,
            device_id_type=MESH,
        )

    def pair_back(rr):
        where = pl.ds(c * half + rr * quarter, quarter)
        return pltpu.make_async_remote_copy(
            src_ref=total.at[where],
            dst_ref=total.at[where],
            send_sem=pair_send.at[1],
            recv_sem=pair_recv.at[1],
            device_id=near_x,
            device_id_type=MESH,
        )

    def core_back(cc):
        where = pl.ds(cc * half, half)
        return pltpu.make_async_remote_copy(
            src_ref=total.at[where],
            dst_ref=total.at[where],
            send_sem=core_send.at[1],
            recv_sem=core_recv.at[1],
            device_id=near_core,
            device_id_type=MESH,
        )

    def make_terms():
        loads[2].wait()
        loads[3].wait()
        for n, operand in enumerate((features_v, aggregated_v)):
            terms[n * half : (n + 1) * half, :] = lax.dot_general(
                operand[...],
                grad_v[...],
                (((0,), (0,)), ((), ())),
                preferred_element_type=jnp.float32,
            )
        core_copy().start()

    def over_cores():
        core_copy().wait_recv()
        half_sum[...] = terms[pl.ds(pl.multiple_of(c * half, half), half), :] + from_core[...]
        pair_copy().start()

    def over_pair():
        pair_copy().wait_recv()
        quarter_sum[...] = (
            half_sum[pl.ds(pl.multiple_of(r * quarter, quarter), quarter), :] + from_x[...]
        )

        @pl.loop(1, seats)
        def _(step):
            part_copy(step, seat).start()

    def over_plane():
        from_plane[seat] = quarter_sum[pl.ds(pl.multiple_of(seat * part, part), part), :]

        @pl.loop(1, seats)
        def _(step):
            part_copy(step, seat_device(step)[0]).wait_recv()

        where = pl.ds(pl.multiple_of(c * half + r * quarter + seat * part, part), part)
        total[where, :] = jnp.sum(from_plane[...], axis=0) * scale

        @pl.loop(1, seats)
        def _(step):
            share_copy(step, seat).start()

    def back_over_pair():
        @pl.loop(1, seats)
        def _(step):
            share_copy(step, seat_device(step)[0]).wait_recv()

        pair_back(r).start()

    def back_over_cores():
        pair_back(1 - r).wait_recv()
        core_back(c).start()

    def self_part():
        loads[9].wait()

        @pl.loop(0, pieces)
        def _(h):
            where = pl.ds(pl.multiple_of(h * piece_rows, piece_rows), piece_rows)
            base_v[where, :] = lax.dot_general(
                grad_v[where, :],
                w_self_v[...],
                (((1,), (1,)), ((), ())),
                preferred_element_type=jnp.float32,
            )

    for h in range(pieces):
        x_copy(h).start()
        pass_on(b, r, h, has_up, has_down, always)

    last = 2 * (line - 1) + 1
    events = [
        (0.1, make_terms),
        (0.2, chain_links),
        (0.3, lambda: links_copy().start()),
        (0.9, over_cores),
        (1.0, from_across),
        (1.45, lambda: (links_copy().wait(), loads[10].wait())),
        (1.9, over_pair),
        (2.9, self_part),
        (3.9, over_plane),
        (5.9, back_over_pair),
        (6.7, back_over_cores),
    ]
    for which in range(2):
        events.append((1.1 + which, functools.partial(from_y, 0, which)))
        for d in range(1, line):
            when = 2 * (d - 1) + 1 + which
            events.append((when, functools.partial(own_line, d, which)))
            if which == 0 or d < line - 1:
                late = min(when + 3, last + (d == line - 1) * 0.8) + 0.05
                events.append((late, functools.partial(from_y, d, which)))
    for d in range(1, line):
        events.append((2 * d + 1 + (d == line - 1) * 0.8, functools.partial(end_line, d)))
    for group in order:
        events.append((ends[group], functools.partial(multiply, group)))
    for _, event in sorted(events, key=lambda pair: pair[0]):
        event()

    def back_copy():
        return pltpu.make_async_remote_copy(
            src_ref=back,
            dst_ref=got_ref,
            send_sem=back_send,
            recv_sem=back_recv,
            device_id=near_x,
            device_id_type=MESH,
        )

    for t in range(share_tiles):
        row = (1 - r) * share_tiles + t
        back[t * side : (t + 1) * side, :] = chain[links_s[1, 0, row]].astype(back.dtype)
    own_half = pl.ds(pl.multiple_of(r * width, width), width)
    for t in range(share_tiles):
        if t == 1:
            back_copy().start()
        row = r * share_tiles + t
        base_v[t * side : (t + 1) * side, own_half] += chain[links_s[1, 0, row]]
    base_copy = local(base_v, base_ref, 12)
    base_copy.start()
    core_back(1 - c).wait_recv()
    sum_copy = local(total, sum_ref, 13)
    sum_copy.start()

    core_copy().wait_send()
    pair_copy().wait_send()
    pair_back(r).wait_send()
    core_back(c).wait_send()

    @pl.loop(1, seats)
    def _(step):
        part_copy(step, seat).wait_send()
        share_copy(step, seat).wait_send()

    @pl.loop(0, pieces)
    def _(h):
        x_copy(h).wait_send()

        @pl.loop(0, line)
        def _(zz):
            for which in range(2):
                share = share_of(which)
                block = zz * plane + y * CORES + c
                beyond = zz * plane + (1 - y) * CORES + c
                special = end_of(zz) if which else never
                goes_up = (zz <= z) & has_up
                goes_down = (zz >= z) & has_down

                @pl.when(goes_up)
                def _():
                    send(block, share, h, 0, up).wait_send()

                @pl.when(goes_down)
                def _():
                    send(block, share, h, 1, down).wait_send()

                @pl.when(jnp.logical_not(special) | (zz == z))
                def _():
                    send(block, share, h, 2, near_y).wait_send()

                send(block, share, h, 3, near_core).wait_send()

                @pl.when(special & goes_up)
                def _():
                    send(beyond, share, h, 0, up).wait_send()

                @pl.when(special & goes_down)
                def _():
                    send(beyond, share, h, 1, down).wait_send()

                send(beyond, share, h, 3, near_core).wait_send()

    sum_copy.wait()
    base_copy.wait()
    back_copy().wait_send()
    back_copy().wait_recv()


def layer(rows, cols, counts, features, aggregated, grad, w_self, w_neigh, tiles, scale, blocks, copies):
    share_rows, width = grad.shape
    half = width // copies
    _, slots, side, _ = tiles.shape
    line = blocks // (CORES * ROWS_Y)
    seats = line * ROWS_Y
    piece_rows = share_rows // PIECES
    count = 2 * CORES * (2 * line - 1)
    bf16, f32, i32 = jnp.bfloat16, jnp.float32, jnp.int32
    dma = pltpu.SemaphoreType.DMA
    operands = (rows, cols, counts, features, aggregated, grad, w_self, w_neigh, tiles)
    return pl.pallas_call(
        functools.partial(layer_kernel, blocks, copies, scale),
        out_shape=(
            jax.ShapeDtypeStruct((share_rows, width), f32),
            jax.ShapeDtypeStruct((share_rows, half), bf16),
            jax.ShapeDtypeStruct((2 * width, width), f32),
        ),
        in_specs=[pl.BlockSpec(memory_space=pl.ANY)] * 9,
        out_specs=(pl.BlockSpec(memory_space=pl.ANY),) * 3,
        scratch_shapes=[
            pltpu.VMEM(rows.shape, i32),
            pltpu.VMEM(counts.shape, i32),
            pltpu.SMEM(rows.shape, i32),
            pltpu.SMEM(cols.shape, i32),
            pltpu.SMEM(counts.shape, i32),
            pltpu.VMEM(features.shape, bf16),
            pltpu.VMEM(aggregated.shape, bf16),
            pltpu.VMEM(grad.shape, bf16),
            pltpu.VMEM(w_self.shape, bf16),
            pltpu.VMEM(w_neigh.shape, bf16),
            pltpu.VMEM(tiles.shape, bf16),
            pltpu.VMEM((blocks, copies, PIECES, piece_rows, half), bf16),
            pltpu.VMEM((PIECES, piece_rows, half), bf16),
            pltpu.VMEM((count, copies * share_rows // side, side, half), bf16),
            pltpu.VMEM((count * slots + 1, side, half), f32),
            pltpu.VMEM((2, *rows.shape), i32),
            pltpu.SMEM((2, *rows.shape), i32),
            pltpu.VMEM((share_rows, width), f32),
            pltpu.VMEM((share_rows, half), bf16),
            pltpu.VMEM((2 * width, width), f32),
            pltpu.VMEM((width, width), f32),
            pltpu.VMEM((width, width), f32),
            pltpu.VMEM((width // 2, width), f32),
            pltpu.VMEM((width // 2, width), f32),
            pltpu.VMEM((seats, width // 2 // seats, width), f32),
            pltpu.VMEM((2 * width, width), f32),
            dma((14,)),
            dma((4, blocks, copies, PIECES)),
            dma((blocks, copies, PIECES)),
            dma((PIECES,)),
            dma,
            dma,
            dma((2,)),
            dma((2,)),
            dma((2,)),
            dma((2,)),
            dma((2, seats)),
            dma((2, seats)),
        ],
        compiler_params=pltpu.CompilerParams(collective_id=0, has_side_effects=True, vmem_limit_bytes=48 << 20),
    )(*(pltpu.with_memory_space_constraint(operand, pltpu.HBM) for operand in operands))


def by_columns(
    features, aggregated, out_grad, w_self, w_neigh, tiles, tile_rows, tile_cols, tile_counts
):
    blocks, copies = lax.axis_size("blk"), lax.axis_size("rep")
    r = lax.axis_index("rep")
    rows, width = out_grad.shape
    half = width // copies
    scale = (rows * blocks * copies) ** (-0.5)
    base, got, sums = layer(
        tile_rows[0].T,
        tile_cols[0].T,
        tile_counts,
        features,
        aggregated,
        out_grad,
        w_self,
        w_neigh,
        tiles[0],
        scale,
        blocks,
        copies,
    )
    other = (jnp.arange(width, dtype=jnp.int32) // half)[None, :] != r
    got = jnp.concatenate([got, got], axis=1).astype(jnp.float32)
    feature_grad = base + jnp.where(other, got, jnp.zeros_like(got))
    return (feature_grad, sums[:width], sums[width:])


def on_device(
    features, aggregated, out_grad, w_self, w_neigh, tiles, tile_rows, tile_cols, tile_counts
):
    block_total = lax.axis_size("blk")
    copies = lax.axis_size("rep")
    replica = lax.axis_index("rep")
    width = out_grad.shape[1]
    side = tiles.shape[-1]
    slots_total = tiles.shape[2]
    share = jnp.dot(out_grad, w_neigh.T, preferred_element_type=jnp.float32).astype(jnp.bfloat16)
    whole = lax.all_gather(share, "rep", axis=0, tiled=True)
    block_rows = whole.shape[0]
    tiles_side = block_rows // side
    pieces_whole = whole.reshape(tiles_side, side, width)
    per_copy = (slots_total + copies - 1) // copies
    slot_ids = replica + copies * jnp.arange(per_copy, dtype=jnp.int32)
    valid = slot_ids < slots_total
    safe = jnp.minimum(slot_ids, slots_total - 1)
    wanted = jnp.take(tile_cols[0], safe, axis=1)
    found = pieces_whole[lax.all_to_all(wanted, "blk", split_axis=0, concat_axis=0, tiled=True)]
    fetched = lax.all_to_all(found, "blk", split_axis=0, concat_axis=0, tiled=True)
    chosen_tiles = jnp.take(tiles[0], safe, axis=1)
    products = jnp.einsum(
        "ikpq,ikqf->ikpf", chosen_tiles, fetched, preferred_element_type=jnp.float32
    )
    live = valid[None, :] & (slot_ids[None, :] < tile_counts[0][:, None])
    products = jnp.where(live[:, :, None, None], products, jnp.zeros_like(products))
    target_rows = jnp.take(tile_rows[0], safe, axis=1).reshape(-1)
    accumulated = jnp.zeros((tiles_side, side, width), jnp.float32)
    accumulated = accumulated.at[target_rows].add(products.reshape(-1, side, width))
    flat = accumulated.reshape(block_rows, width)
    self_part = jnp.dot(out_grad, w_self.T, preferred_element_type=jnp.float32)
    contract = (((0,), (0,)), ((), ()))
    terms_self = lax.dot_general(features, out_grad, contract, preferred_element_type=jnp.float32)
    terms_neigh = lax.dot_general(
        aggregated, out_grad, contract, preferred_element_type=jnp.float32
    )
    scale = (out_grad.shape[0] * block_total * copies) ** (-0.5)
    spread_share = lax.psum_scatter(flat, "rep", scatter_dimension=0, tiled=True)
    self_sum, neigh_sum = lax.psum((terms_self, terms_neigh), ("blk", "rep"))
    return (spread_share + self_part, self_sum * scale, neigh_sum * scale)


def solution(mesh):
    blocks, copies = mesh.shape["blk"], mesh.shape["rep"]
    by_pairs = copies == 2 and blocks % (CORES * ROWS_Y) == 0
    placed = (
        P(("blk", "rep"), None),
        P(("blk", "rep"), None),
        P(("blk", "rep"), None),
        P(),
        P(),
        P("blk", None, None, None, None),
        P("blk", None, None),
        P("blk", None, None),
        P("blk", None),
    )
    return jax.shard_map(
        by_columns if by_pairs else on_device,
        mesh=mesh,
        in_specs=placed,
        out_specs=(P(("blk", "rep"), None), P(), P()),
        check_vma=False,
    )
```

profile of v0, /device:TPU:0, one launch (start us, length us, event | category | flops | bytes accessed | tf_op | source)
XLA Modules:
  0.0 65.2 jit_solution(5003175520090524422)
XLA Ops:
  0.6 62.6 %shard_map.112 = (f32[1024,256]{1,0:T(8,128)S(1)}, bf16[1024,128]{1,0:T(8,128)(2,1)S(1)}, f32[512,256]{1,0:T(8,128)S(1)}) custom-call(s32[8,16]{1,0:T(8,128)} %bitcast.8, s32[8,16]{1,0:T(8,128)} %bitcast.9, s32[1,16]{1,0:T(1,128)} %counts_ref.1, bf16[1024,256]{1,0:T(8,128)(2,1)} %features_ref.1, bf16[1024,256]{1,0:T(8,128)(2,1)} %aggregated_ref.1, ...), custom_call_target="tpu_custom_call" | custom-call | tf_op jit(solution)/shard_map/pallas_call | solution.py:622
  63.3 1.1 %select_add_fusion = f32[1024,256]{1,0:T(8,128)} fusion(f32[1024,256]{1,0:T(8,128)S(1)} %get-tuple-element.6, bf16[1024,128]{1,0:T(8,128)(2,1)S(1)} %get-tuple-element.7, pred[256]{0:T(512)(128)(4,1)S(1)} %fusion), kind=kLoop, calls=%fused_computation | loop fusion | flops 1572864 | bytes 2359552 | tf_op jit(solution)/shard_map/add | solution.py:699
  64.4 0.8 %fusion.1 = (f32[256,256]{1,0:T(8,128)}, f32[256,256]{1,0:T(8,128)}) fusion(f32[512,256]{1,0:T(8,128)S(1)} %get-tuple-element.8), kind=kLoop, calls=%fused_computation.6 | loop fusion | bytes 1048576 | tf_op jit(solution)/shard_map/slice | solution.py:700
  (1 shorter events, 0.0 us)
where the time goes:
time: 65.4 us; the launch traced here: 65.2 us
  Pallas kernels  62.6 us (96%)
  other arithmetic  1.09 us (2%)
  local copies, waits for them, and re-layouts  0.82 us (1%)
    pallas_call x1, Pallas kernels, layer(): pl.pallas_call(functools.partial(layer_kernel, blocks, copies, scale), ou...  62.6 us

commit v1 on v0

--- a/solution.py
+++ b/solution.py
@@ -364,7 +364,9 @@
 
     out_width = total.shape[1]
     half, quarter = total.shape[0] // 2, total.shape[0] // 4
-    part = quarter // seats
+    first_owner, owners = (ROWS_Y, seats - 2 * ROWS_Y) if line > 2 else (0, seats)
+    part = quarter // owners
+    owns = (seat >= first_owner) & (seat < first_owner + owners)
 
     def core_copy():
         return pltpu.make_async_remote_copy(
@@ -386,20 +388,29 @@
             device_id_type=MESH,
         )
 
-    def part_copy(step, slot):
-        other, device = seat_device(step)
-        return pltpu.make_async_remote_copy(
-            src_ref=quarter_sum.at[pl.ds(other * part, part)],
+    def part_of(owner):
+        return pl.multiple_of((owner - first_owner) * part, part)
+
+    def part_copy(owner, slot):
+        return pltpu.make_async_remote_copy(
+            src_ref=quarter_sum.at[pl.ds(part_of(owner), part)],
             dst_ref=from_plane.at[slot],
-            send_sem=plane_send.at[0, other],
+            send_sem=plane_send.at[0, owner],
             recv_sem=plane_recv.at[0, slot],
-            device_id=device,
-            device_id_type=MESH,
-        )
-
-    def share_copy(step, owner):
-        other, device = seat_device(step)
-        where = pl.ds(c * half + r * quarter + owner * part, part)
+            device_id=seat_device(owner - seat + seats)[1],
+            device_id_type=MESH,
+        )
+
+    def others(first, count, act):
+        @pl.loop(first, first + count)
+        def _(other):
+            @pl.when(other != seat)
+            def _():
+                act(other)
+
+    def share_copy(other, owner):
+        device = seat_device(other - seat + seats)[1]
+        where = pl.ds(c * half + r * quarter + part_of(owner), part)
         return pltpu.make_async_remote_copy(
             src_ref=total.at[where],
             dst_ref=total.at[where],
@@ -454,29 +465,19 @@
             half_sum[pl.ds(pl.multiple_of(r * quarter, quarter), quarter), :] + from_x[...]
         )
 
-        @pl.loop(1, seats)
-        def _(step):
-            part_copy(step, seat).start()
+        others(first_owner, owners, lambda other: part_copy(other, seat).start())
 
     def over_plane():
-        from_plane[seat] = quarter_sum[pl.ds(pl.multiple_of(seat * part, part), part), :]
-
-        @pl.loop(1, seats)
-        def _(step):
-            part_copy(step, seat_device(step)[0]).wait_recv()
-
-        where = pl.ds(pl.multiple_of(c * half + r * quarter + seat * part, part), part)
-        total[where, :] = jnp.sum(from_plane[...], axis=0) * scale
-
-        @pl.loop(1, seats)
-        def _(step):
-            share_copy(step, seat).start()
+        @pl.when(owns)
+        def _():
+            from_plane[seat] = quarter_sum[pl.ds(part_of(seat), part), :]
+            others(0, seats, lambda other: part_copy(seat, other).wait_recv())
+            where = pl.ds(pl.multiple_of(c * half + r * quarter + part_of(seat), part), part)
+            total[where, :] = jnp.sum(from_plane[...], axis=0) * scale
+            others(0, seats, lambda other: share_copy(other, seat).start())
 
     def back_over_pair():
-        @pl.loop(1, seats)
-        def _(step):
-            share_copy(step, seat_device(step)[0]).wait_recv()
-
+        others(first_owner, owners, lambda other: share_copy(seat, other).wait_recv())
         pair_back(r).start()
 
     def back_over_cores():
@@ -559,10 +560,11 @@
     pair_back(r).wait_send()
     core_back(c).wait_send()
 
-    @pl.loop(1, seats)
-    def _(step):
-        part_copy(step, seat).wait_send()
-        share_copy(step, seat).wait_send()
+    others(first_owner, owners, lambda other: part_copy(other, seat).wait_send())
+
+    @pl.when(owns)
+    def _():
+        others(0, seats, lambda other: share_copy(other, seat).wait_send())
 
     @pl.loop(0, pieces)
     def _(h):
@@ -615,6 +617,7 @@
     line = blocks // (CORES * ROWS_Y)
     seats = line * ROWS_Y
     piece_rows = share_rows // PIECES
+    owners = seats - 2 * ROWS_Y if line > 2 else seats
     count = 2 * CORES * (2 * line - 1)
     bf16, f32, i32 = jnp.bfloat16, jnp.float32, jnp.int32
     dma = pltpu.SemaphoreType.DMA
@@ -653,7 +656,7 @@
             pltpu.VMEM((width, width), f32),
             pltpu.VMEM((width // 2, width), f32),
             pltpu.VMEM((width // 2, width), f32),
-            pltpu.VMEM((seats, width // 2 // seats, width), f32),
+            pltpu.VMEM((seats, width // 2 // owners, width), f32),
             pltpu.VMEM((2 * width, width), f32),
             dma((14,)),
             dma((4, blocks, copies, PIECES)),

time: 65.4 us -> 64 us (0.979)
  Pallas kernels: 62.6 us -> 61.2 us
    pallas_call x1, Pallas kernels: 62.6 us -> 61.2 us  [layer(): pl.pallas_call(functools.partial(layer_kernel, blocks, copies, scale), ou...]
where the time goes in v1:
time: 64 us; the launch traced here: 63.8 us
  Pallas kernels  61.2 us (96%)
  other arithmetic  1.09 us (2%)
  local copies, waits for them, and re-layouts  0.82 us (1%)
  between operations  0.65 us (1%)
    pallas_call x1, Pallas kernels, layer(): pl.pallas_call(functools.partial(layer_kernel, blocks, copies, scale), ou...  61.2 us

profile of v1, /device:TPU:0, one launch (start us, length us, event | category | flops | bytes accessed | tf_op | source)
XLA Modules:
  0.0 63.8 jit_solution(15408855171507692090)
XLA Ops:
  0.6 61.2 %shard_map.112 = (f32[1024,256]{1,0:T(8,128)S(1)}, bf16[1024,128]{1,0:T(8,128)(2,1)S(1)}, f32[512,256]{1,0:T(8,128)S(1)}) custom-call(s32[8,16]{1,0:T(8,128)} %bitcast.8, s32[8,16]{1,0:T(8,128)} %bitcast.9, s32[1,16]{1,0:T(1,128)} %counts_ref.1, bf16[1024,256]{1,0:T(8,128)(2,1)} %features_ref.1, bf16[1024,256]{1,0:T(8,128)(2,1)} %aggregated_ref.1, ...), custom_call_target="tpu_custom_call" | custom-call | tf_op jit(solution)/shard_map/pallas_call | solution.py:625
  61.9 1.1 %select_add_fusion = f32[1024,256]{1,0:T(8,128)} fusion(f32[1024,256]{1,0:T(8,128)S(1)} %get-tuple-element.6, bf16[1024,128]{1,0:T(8,128)(2,1)S(1)} %get-tuple-element.7, pred[256]{0:T(512)(128)(4,1)S(1)} %fusion), kind=kLoop, calls=%fused_computation | loop fusion | flops 1572864 | bytes 2359552 | tf_op jit(solution)/shard_map/add | solution.py:702
  63.0 0.8 %fusion.1 = (f32[256,256]{1,0:T(8,128)}, f32[256,256]{1,0:T(8,128)}) fusion(f32[512,256]{1,0:T(8,128)S(1)} %get-tuple-element.8), kind=kLoop, calls=%fused_computation.6 | loop fusion | bytes 1048576 | tf_op jit(solution)/shard_map/slice | solution.py:703
  (1 shorter events, 0.0 us)

commit v2 on v1

--- a/solution.py
+++ b/solution.py
@@ -11,20 +11,38 @@
 CORES, ROWS_Y = 2, 2
 
 
-PIECES = 2
-
-
-def positions(line):
-    last = 2 * (line - 1) + 1
-    own = lambda d, w: 2 * (d - 1) + 1 + w if d else w
-    ends = {}
-    for d in range(line):
-        ends[d, 0, 0] = own(d, 1) + 0.5
-        ends[d, 1, 0] = 2.5 if d == 0 else min(own(d, 1) + 3, last + (d == line - 1) * 0.8) + 0.1
-    for d in range(line):
-        for other in range(2):
-            ends[d, other, 1] = ends[d, other, 0] + (0.1 if ends[d, other, 0] > last else 0.95)
-    return ends
+CHUNKS = 2
+
+
+def schedule(line):
+    last = line - 1
+    own, across, ends, uses = {}, {}, {}, {}
+    for h in range(CHUNKS):
+        for w in range(2):
+            across[0, w, h] = 1.1 + w + 0.01 * h
+            own[1, w, h] = 1 + w + 0.01 * h
+            across[1, w, h] = 4.05 + 0.5 * w + 0.01 * h
+            for d in range(2, line):
+                later = w + h if d == last else w + 1.05 * h
+                own[d, w, h] = 2 * d - 1.5 + (later if w == 0 or d < last else 0.5 + 1.5 * h)
+                across[d, w, h] = 2 * d + (h + 0.1 if d == last else 1.55 + 0.05 * w + (0.5 + 0.5 * w) * h)
+        ends[1, h] = 3 + 0.01 * h
+        for d in range(2, line):
+            ends[d, h] = 2 * d + (h + 0.05 if d == last else 0.5 + 0.5 * h)
+        for d in range(line):
+            uses[d, 0, 0, h] = max(own[d, 1, h] if d else 1.0, 1.5) + 0.03
+            uses[d, 1, 0, h] = (
+                0.03
+                + max(
+                    [across[d, 0, h]]
+                    + ([across[d, 1, h]] if d < last else [])
+                    + ([ends[d, h]] if d else [])
+                )
+            )
+            for other in range(2):
+                when = uses[d, other, 0, h]
+                uses[d, other, 1, h] = when + (0.45 if when < 2 * last else 0.1)
+    return own, across, ends, uses
 
 
 def layer_kernel(
@@ -40,8 +58,7 @@
     w_self_ref,
     w_neigh_ref,
     tiles_ref,
-    base_ref,
-    got_ref,
+    base_v,
     sum_ref,
     rows_v,
     counts_v,
@@ -60,8 +77,8 @@
     chain,
     links_v,
     links_s,
-    base_v,
     back,
+    got,
     terms,
     from_core,
     half_sum,
@@ -94,9 +111,11 @@
     has_up, has_down = z < line - 1, z > 0
     never = z < 0
     always = z >= 0
-    pieces, piece_rows, width = g.shape[2:]
+    chunks, chunk_rows, width = g.shape[2:]
     slots, side = tiles_v.shape[1], tiles_v.shape[2]
-    share_tiles = pieces * piece_rows // side
+    share_tiles = chunks * chunk_rows // side
+    packed_tiles = chunk_rows // side
+    of_lane = lax.broadcasted_iota(jnp.int32, (side, width), 1) // (width // chunks)
     seats = line * ROWS_Y
     seat = z * ROWS_Y + y
     end_of = lambda zz: (zz == 0) | (zz == line - 1)
@@ -139,17 +158,26 @@
     loads[0].wait()
     loads[1].wait()
 
+    features_each = width // chunks
+
     def message(which, h):
-        return lax.dot_general(
-            grad_v[pl.ds(h * piece_rows, piece_rows), :],
-            w_neigh_v[pl.ds(pl.multiple_of(which * width, width), width), :],
-            (((1,), (1,)), ((), ())),
-            preferred_element_type=jnp.float32,
-        ).astype(g.dtype)
-
-    for h in range(pieces):
+        first = pl.multiple_of(which * width + h * features_each, features_each)
+        chosen = w_neigh_v[pl.ds(first, features_each), :]
+        blank = jnp.zeros_like(chosen)
+        packed = [
+            lax.dot_general(
+                grad_v[q * chunk_rows : (q + 1) * chunk_rows, :],
+                jnp.concatenate([chosen if n == q else blank for n in range(chunks)], axis=0),
+                (((1,), (1,)), ((), ())),
+                preferred_element_type=jnp.float32,
+            )
+            for q in range(chunks)
+        ]
+        return sum(packed[1:], packed[0]).astype(g.dtype)
+
+    for h in range(chunks):
         g[b, r, h] = message(r, h)
-    for h in range(pieces):
+    for h in range(chunks):
         across[h] = message(1 - r, h)
 
     pl.semaphore_wait(barrier, 2 + seats - 1)
@@ -198,81 +226,76 @@
     def there(zz):
         return (zz >= 0) & (zz < line)
 
-    def own_line(d, which):
+    def own_line(d, which, h):
         share = share_of(which)
 
-        @pl.loop(0, pieces)
-        def _(h):
-            for sign in (-1, 1):
-                zz = z + sign * d
-
-                @pl.when(there(zz))
-                def _():
-                    block = zz * plane + y * CORES + c
-                    arrived(block, share, h)
-                    pass_on(
-                        block,
-                        share,
-                        h,
-                        has_up if sign < 0 else never,
-                        has_down if sign > 0 else never,
-                        jnp.logical_not(end_of(zz)) if which else always,
-                    )
-
-    def from_across():
-        @pl.loop(0, pieces)
-        def _(h):
-            arrived(b, 1 - r, h)
-            pass_on(b, 1 - r, h, has_up, has_down, always)
-
-    def from_y(d, which):
+        for sign in (-1, 1):
+            zz = z + sign * d
+
+            @pl.when(there(zz))
+            def _():
+                block = zz * plane + y * CORES + c
+                arrived(block, share, h)
+                pass_on(
+                    block,
+                    share,
+                    h,
+                    has_up if sign < 0 else never,
+                    has_down if sign > 0 else never,
+                    jnp.logical_not(end_of(zz)) if which else always,
+                )
+
+    def from_across(h):
+        arrived(b, 1 - r, h)
+        pass_on(b, 1 - r, h, has_up, has_down, always)
+
+    def from_y(d, which, h):
         share = share_of(which)
 
-        @pl.loop(0, pieces)
-        def _(h):
-            for sign in (-1, 1) if d else (0,):
-                zz = z + sign * d
-                wanted = there(zz)
-                if which and d:
-                    wanted = wanted & jnp.logical_not(end_of(zz))
-
-                @pl.when(wanted)
-                def _():
-                    block = zz * plane + (1 - y) * CORES + c
-                    arrived(block, share, h)
-                    onward = which == 1 and d == 0
-                    pass_on(
-                        block,
-                        share,
-                        h,
-                        has_up & (z == 0) if onward else never,
-                        has_down & (z == line - 1) if onward else never,
-                        never,
-                    )
-
-    def end_line(d):
+        for sign in (-1, 1) if d else (0,):
+            zz = z + sign * d
+            wanted = there(zz)
+            if which and d:
+                wanted = wanted & jnp.logical_not(end_of(zz))
+
+            @pl.when(wanted)
+            def _():
+                block = zz * plane + (1 - y) * CORES + c
+                arrived(block, share, h)
+                onward = which == 1 and d == 0
+                pass_on(
+                    block,
+                    share,
+                    h,
+                    has_up & (z == 0) if onward else never,
+                    has_down & (z == line - 1) if onward else never,
+                    never,
+                )
+
+    def end_line(d, h):
         share = share_of(1)
 
-        @pl.loop(0, pieces)
-        def _(h):
-            for sign in (-1, 1):
-                zz = z + sign * d
-
-                @pl.when(there(zz) & end_of(zz))
-                def _():
-                    block = zz * plane + (1 - y) * CORES + c
-                    arrived(block, share, h)
-                    pass_on(
-                        block,
-                        share,
-                        h,
-                        has_up if sign < 0 else never,
-                        has_down if sign > 0 else never,
-                        never,
-                    )
-
-    ends = positions(line)
-    order = sorted(ends, key=lambda group: (ends[group], group))
+        for sign in (-1, 1):
+            zz = z + sign * d
+
+            @pl.when(there(zz) & end_of(zz))
+            def _():
+                block = zz * plane + (1 - y) * CORES + c
+                arrived(block, share, h)
+                pass_on(
+                    block,
+                    share,
+                    h,
+                    has_up if sign < 0 else never,
+                    has_down if sign > 0 else never,
+                    never,
+                )
+
+    own_times, y_times, end_times, use_times = schedule(line)
+    order = sorted(
+        (group[:3] for group in use_times if group[3] == 0),
+        key=lambda group: (use_times[(*group, 0)], group),
+    )
     starts, count = {}, 0
     for group in order:
         starts[group] = count
@@ -318,12 +341,13 @@
         before, last = lax.fori_loop(0, slots, step, (none, none))
         links_v[0] = jnp.where(before < 0, nothing, before)
         links_v[1] = jnp.where(last < 0, nothing, last)
-        chain[nothing] = jnp.zeros(chain.shape[1:], chain.dtype)
+        for h in range(chunks):
+            chain[h, nothing] = jnp.zeros(chain.shape[2:], chain.dtype)
 
     def links_copy():
         return local(links_v, links_s, 11)
 
-    def multiply(group):
+    def multiply(group, h):
         d, other_y, other_core = group
         first = starts[group]
 
@@ -334,25 +358,23 @@
             def _():
                 block = block_of(zz, other_y, other_core)
                 if other_core:
-
-                    @pl.loop(0, pieces)
-                    def _(h):
-                        for share in range(copies):
-                            arrived(block, share, h)
+                    for share in range(copies):
+                        arrived(block, share, h)
 
                 seat_of = first + i
-                current[seat_of] = g[block].reshape(current.shape[1:])
+                for share in range(copies):
+                    current[seat_of, share] = g[block, share, h].reshape(current.shape[2:])
                 products = []
                 for k in range(slots):
+                    column = cols_s[k, block]
+                    share, within = column // share_tiles, column % share_tiles
+                    piece = current[seat_of, share, within % packed_tiles]
+                    piece = jnp.where(of_lane == within // packed_tiles, piece, jnp.zeros_like(piece))
                     products.append(
-                        jnp.dot(
-                            tiles_v[block, k],
-                            current[seat_of, cols_s[k, block]],
-                            preferred_element_type=jnp.float32,
-                        )
+                        jnp.dot(tiles_v[block, k], piece, preferred_element_type=jnp.float32)
                     )
                 for k in range(slots):
-                    chain[seat_of * slots + k] = products[k] + chain[links_s[0, k, block]]
+                    chain[h, seat_of * slots + k] = products[k] + chain[h, links_s[0, k, block]]
 
         if d:
 
@@ -487,9 +509,9 @@
     def self_part():
         loads[9].wait()
 
-        @pl.loop(0, pieces)
+        @pl.loop(0, chunks)
         def _(h):
-            where = pl.ds(pl.multiple_of(h * piece_rows, piece_rows), piece_rows)
+            where = pl.ds(pl.multiple_of(h * chunk_rows, chunk_rows), chunk_rows)
             base_v[where, :] = lax.dot_general(
                 grad_v[where, :],
                 w_self_v[...],
@@ -497,62 +519,89 @@
                 preferred_element_type=jnp.float32,
             )
 
-    for h in range(pieces):
+    for h in range(chunks):
         x_copy(h).start()
         pass_on(b, r, h, has_up, has_down, always)
 
-    last = 2 * (line - 1) + 1
+    def back_copy(h):
+        return pltpu.make_async_remote_copy(
+            src_ref=back.at[h],
+            dst_ref=got.at[h],
+            send_sem=back_send.at[h],
+            recv_sem=back_recv.at[h],
+            device_id=near_x,
+            device_id_type=MESH,
+        )
+
+    own_half = pl.ds(pl.multiple_of(r * width, width), width)
+    other_half = pl.ds(pl.multiple_of((1 - r) * width, width), width)
+
+    def turned(value):
+        return pltpu.roll(value, width // chunks, 1)
+
+    def whole(h, row):
+        value = chain[h, links_s[1, 0, row]]
+        return value + turned(value)
+
+    def give_back(h):
+        for t in range(packed_tiles):
+            row = (1 - r) * share_tiles + t
+            low, high = whole(h, row), whole(h, row + packed_tiles)
+            back[h, t * side : (t + 1) * side, :] = jnp.where(of_lane == 0, low, high).astype(
+                back.dtype
+            )
+
+    def keep(h):
+        for t in range(share_tiles):
+            if t == 1:
+                back_copy(h).start()
+            value = whole(h, r * share_tiles + t)
+            value = jnp.where(of_lane == h, value, jnp.zeros_like(value))
+            base_v[t * side : (t + 1) * side, own_half] += value
+
+    def take(h):
+        back_copy(h).wait_recv()
+        for t in range(packed_tiles):
+            value = got[h, t * side : (t + 1) * side, :].astype(jnp.float32)
+            other = turned(value)
+            for q in range(chunks):
+                chosen = value if q == h else other
+                chosen = jnp.where(of_lane == h, chosen, jnp.zeros_like(chosen))
+                first = (t + q * packed_tiles) * side
+                base_v[first : first + side, other_half] += chosen
+
     events = [
         (0.1, make_terms),
         (0.2, chain_links),
         (0.3, lambda: links_copy().start()),
         (0.9, over_cores),
-        (1.0, from_across),
         (1.45, lambda: (links_copy().wait(), loads[10].wait())),
         (1.9, over_pair),
         (2.9, self_part),
         (3.9, over_plane),
         (5.9, back_over_pair),
-        (6.7, back_over_cores),
+        (6.65, back_over_cores),
     ]
-    for which in range(2):
-        events.append((1.1 + which, functools.partial(from_y, 0, which)))
-        for d in range(1, line):
-            when = 2 * (d - 1) + 1 + which
-            events.append((when, functools.partial(own_line, d, which)))
-            if which == 0 or d < line - 1:
-                late = min(when + 3, last + (d == line - 1) * 0.8) + 0.05
-                events.append((late, functools.partial(from_y, d, which)))
-    for d in range(1, line):
-        events.append((2 * d + 1 + (d == line - 1) * 0.8, functools.partial(end_line, d)))
-    for group in order:
-        events.append((ends[group], functools.partial(multiply, group)))
+    for h in range(chunks):
+        events.append((1.0 + 0.01 * h, functools.partial(from_across, h)))
+    for act, times in ((own_line, own_times), (from_y, y_times), (end_line, end_times)):
+        for key, when in times.items():
+            if act is not from_y or key[:2] != (line - 1, 1):
+                events.append((when, functools.partial(act, *key)))
+    for h in range(chunks):
+        when = 0
+        for group in order:
+            when = max(when, use_times[(*group, h)])
+            events.append((when, functools.partial(multiply, group, h)))
+        events.append((when + 0.001, functools.partial(give_back, h)))
+        events.append((when + 0.002, functools.partial(keep, h)))
     for _, event in sorted(events, key=lambda pair: pair[0]):
         event()
 
-    def back_copy():
-        return pltpu.make_async_remote_copy(
-            src_ref=back,
-            dst_ref=got_ref,
-            send_sem=back_send,
-            recv_sem=back_recv,
-            device_id=near_x,
-            device_id_type=MESH,
-        )
-
-    for t in range(share_tiles):
-        row = (1 - r) * share_tiles + t
-        back[t * side : (t + 1) * side, :] = chain[links_s[1, 0, row]].astype(back.dtype)
-    own_half = pl.ds(pl.multiple_of(r * width, width), width)
-    for t in range(share_tiles):
-        if t == 1:
-            back_copy().start()
-        row = r * share_tiles + t
-        base_v[t * side : (t + 1) * side, own_half] += chain[links_s[1, 0, row]]
-    base_copy = local(base_v, base_ref, 12)
-    base_copy.start()
+    for h in range(chunks - 1):
+        take(h)
     core_back(1 - c).wait_recv()
-    sum_copy = local(total, sum_ref, 13)
+    sum_copy = local(total, sum_ref, 12)
     sum_copy.start()
 
     core_copy().wait_send()
@@ -566,7 +615,7 @@
     def _():
         others(0, seats, lambda other: share_copy(other, seat).wait_send())
 
-    @pl.loop(0, pieces)
+    @pl.loop(0, chunks)
     def _(h):
         x_copy(h).wait_send()
 
@@ -605,9 +654,9 @@
                 send(beyond, share, h, 3, near_core).wait_send()
 
     sum_copy.wait()
-    base_copy.wait()
-    back_copy().wait_send()
-    back_copy().wait_recv()
+    for h in range(chunks):
+        back_copy(h).wait_send()
+    take(chunks - 1)
 
 
 def layer(rows, cols, counts, features, aggregated, grad, w_self, w_neigh, tiles, scale, blocks, copies):
@@ -616,7 +665,7 @@
     _, slots, side, _ = tiles.shape
     line = blocks // (CORES * ROWS_Y)
     seats = line * ROWS_Y
-    piece_rows = share_rows // PIECES
+    chunk_rows = share_rows // CHUNKS
     owners = seats - 2 * ROWS_Y if line > 2 else seats
     count = 2 * CORES * (2 * line - 1)
     bf16, f32, i32 = jnp.bfloat16, jnp.float32, jnp.int32
@@ -625,12 +674,14 @@
     return pl.pallas_call(
         functools.partial(layer_kernel, blocks, copies, scale),
         out_shape=(
-            jax.ShapeDtypeStruct((share_rows, width), f32),
-            jax.ShapeDtypeStruct((share_rows, half), bf16),
-            jax.ShapeDtypeStruct((2 * width, width), f32),
+            pltpu.VMEM((share_rows, width), f32),
+            pltpu.VMEM((2 * width, width), f32),
         ),
         in_specs=[pl.BlockSpec(memory_space=pl.ANY)] * 9,
-        out_specs=(pl.BlockSpec(memory_space=pl.ANY),) * 3,
+        out_specs=(
+            pl.BlockSpec(memory_space=pltpu.VMEM),
+            pl.BlockSpec(memory_space=pl.ANY),
+        ),
         scratch_shapes=[
             pltpu.VMEM(rows.shape, i32),
             pltpu.VMEM(counts.shape, i32),
@@ -643,14 +694,14 @@
             pltpu.VMEM(w_self.shape, bf16),
             pltpu.VMEM(w_neigh.shape, bf16),
             pltpu.VMEM(tiles.shape, bf16),
-            pltpu.VMEM((blocks, copies, PIECES, piece_rows, half), bf16),
-            pltpu.VMEM((PIECES, piece_rows, half), bf16),
-            pltpu.VMEM((count, copies * share_rows // side, side, half), bf16),
-            pltpu.VMEM((count * slots + 1, side, half), f32),
+            pltpu.VMEM((blocks, copies, CHUNKS, chunk_rows, half), bf16),
+            pltpu.VMEM((CHUNKS, chunk_rows, half), bf16),
+            pltpu.VMEM((count, copies, chunk_rows // side, side, half), bf16),
+            pltpu.VMEM((CHUNKS, count * slots + 1, side, half), f32),
             pltpu.VMEM((2, *rows.shape), i32),
             pltpu.SMEM((2, *rows.shape), i32),
-            pltpu.VMEM((share_rows, width), f32),
-            pltpu.VMEM((share_rows, half), bf16),
+            pltpu.VMEM((CHUNKS, chunk_rows, half), bf16),
+            pltpu.VMEM((CHUNKS, chunk_rows, half), bf16),
             pltpu.VMEM((2 * width, width), f32),
             pltpu.VMEM((width, width), f32),
             pltpu.VMEM((width, width), f32),
@@ -658,12 +709,12 @@
             pltpu.VMEM((width // 2, width), f32),
             pltpu.VMEM((seats, width // 2 // owners, width), f32),
             pltpu.VMEM((2 * width, width), f32),
-            dma((14,)),
-            dma((4, blocks, copies, PIECES)),
-            dma((blocks, copies, PIECES)),
-            dma((PIECES,)),
-            dma,
-            dma,
+            dma((13,)),
+            dma((4, blocks, copies, CHUNKS)),
+            dma((blocks, copies, CHUNKS)),
+            dma((CHUNKS,)),
+            dma((CHUNKS,)),
+            dma((CHUNKS,)),
             dma((2,)),
             dma((2,)),
             dma((2,)),
@@ -671,7 +722,7 @@
             dma((2, seats)),
             dma((2, seats)),
         ],
-        compiler_params=pltpu.CompilerParams(collective_id=0, has_side_effects=True, vmem_limit_bytes=48 << 20),
+        compiler_params=pltpu.CompilerParams(collective_id=0, has_side_effects=True, vmem_limit_bytes=54 << 20),
     )(*(pltpu.with_memory_space_constraint(operand, pltpu.HBM) for operand in operands))
 
 
@@ -679,11 +730,9 @@
     features, aggregated, out_grad, w_self, w_neigh, tiles, tile_rows, tile_cols, tile_counts
 ):
     blocks, copies = lax.axis_size("blk"), lax.axis_size("rep")
-    r = lax.axis_index("rep")
     rows, width = out_grad.shape
-    half = width // copies
     scale = (rows * blocks * copies) ** (-0.5)
-    base, got, sums = layer(
+    feature_grad, sums = layer(
         tile_rows[0].T,
         tile_cols[0].T,
         tile_counts,
@@ -697,9 +746,6 @@
         blocks,
         copies,
     )
-    other = (jnp.arange(width, dtype=jnp.int32) // half)[None, :] != r
-    got = jnp.concatenate([got, got], axis=1).astype(jnp.float32)
-    feature_grad = base + jnp.where(other, got, jnp.zeros_like(got))
     return (feature_grad, sums[:width], sums[width:])
 
 
@@ -716,13 +762,13 @@
     whole = lax.all_gather(share, "rep", axis=0, tiled=True)
     block_rows = whole.shape[0]
     tiles_side = block_rows // side
-    pieces_whole = whole.reshape(tiles_side, side, width)
+    chunks_whole = whole.reshape(tiles_side, side, width)
     per_copy = (slots_total + copies - 1) // copies
     slot_ids = replica + copies * jnp.arange(per_copy, dtype=jnp.int32)
     valid = slot_ids < slots_total
     safe = jnp.minimum(slot_ids, slots_total - 1)
     wanted = jnp.take(tile_cols[0], safe, axis=1)
-    found = pieces_whole[lax.all_to_all(wanted, "blk", split_axis=0, concat_axis=0, tiled=True)]
+    found = chunks_whole[lax.all_to_all(wanted, "blk", split_axis=0, concat_axis=0, tiled=True)]
     fetched = lax.all_to_all(found, "blk", split_axis=0, concat_axis=0, tiled=True)
     chosen_tiles = jnp.take(tiles[0], safe, axis=1)
     products = jnp.einsum(
@@ -748,7 +794,7 @@
 
 def solution(mesh):
     blocks, copies = mesh.shape["blk"], mesh.shape["rep"]
-    by_pairs = copies == 2 and blocks % (CORES * ROWS_Y) == 0
+    by_pairs = copies == 2 and blocks % (CORES * ROWS_Y) == 0 and blocks > 2 * CORES * ROWS_Y
     placed = (
         P(("blk", "rep"), None),
         P(("blk", "rep"), None),

time: 64 us -> 62.5 us (0.977)
  Pallas kernels: 61.2 us -> 60 us
  other arithmetic: 1.09 us -> 0 us
  local copies, waits for them, and re-layouts: 0.82 us -> 1.8 us
    pallas_call x1, Pallas kernels: 61.2 us -> 60 us  [layer(): pl.pallas_call(functools.partial(layer_kernel, blocks, copies, scale), ou...]
    add x1 -> x0, other arithmetic: 1.08 us -> none  [by_columns(): feature_grad = base + jnp.where(other, got, jnp.zeros_like(got))]
    unnamed x0 -> x1, local copies, waits for them, and re-layouts: none -> 0.97 us
where the time goes in v2:
time: 62.5 us; the launch traced here: 62.4 us
  Pallas kernels  60 us (96%)
  local copies, waits for them, and re-layouts  1.8 us (3%)
  between operations  0.64 us (1%)
    pallas_call x1, Pallas kernels, layer(): pl.pallas_call(functools.partial(layer_kernel, blocks, copies, scale), ou...  60 us

profile of v2, /device:TPU:0, one launch (start us, length us, event | category | flops | bytes accessed | tf_op | source)
XLA Modules:
  0.0 62.4 jit_solution(12525685121595996374)
XLA Ops:
  0.6 60.0 %shard_map.112 = (f32[1024,256]{1,0:T(8,128)S(1)}, f32[512,256]{1,0:T(8,128)S(1)}) custom-call(s32[8,16]{1,0:T(8,128)} %bitcast.8, s32[8,16]{1,0:T(8,128)} %bitcast.9, s32[1,16]{1,0:T(1,128)} %counts_ref.1, bf16[1024,256]{1,0:T(8,128)(2,1)} %features_ref.1, bf16[1024,256]{1,0:T(8,128)(2,1)} %aggregated_ref.1, bf16[1024,256]{1,0:T(8,128)(2,1)} %grad_ref.1, ...), custom_call_target="tpu_custom_call" | custom-call | tf_op jit(solution)/shard_map/pallas_call | solution.py:674
  60.6 1.0 %copy.13 = f32[1024,256]{1,0:T(8,128)} copy(f32[1024,256]{1,0:T(8,128)S(1)} %get-tuple-element.9) | data formatting | bytes 2097152
  61.6 0.8 %fusion = (f32[256,256]{1,0:T(8,128)}, f32[256,256]{1,0:T(8,128)}) fusion(f32[512,256]{1,0:T(8,128)S(1)} %get-tuple-element.6), kind=kLoop, calls=%fused_computation | loop fusion | bytes 1048576 | tf_op jit(solution)/shard_map/slice | solution.py:749

commit v3 on v2

--- a/solution.py
+++ b/solution.py
@@ -59,7 +59,7 @@
     w_neigh_ref,
     tiles_ref,
     base_v,
-    sum_ref,
+    total,
     rows_v,
     counts_v,
     rows_s,
@@ -85,7 +85,6 @@
     from_x,
     quarter_sum,
     from_plane,
-    total,
     local_sem,
     send_sem,
     recv_sem,
@@ -363,12 +362,12 @@
 
                 seat_of = first + i
                 for share in range(copies):
-                    current[seat_of, share] = g[block, share, h].reshape(current.shape[2:])
+                    current[h, seat_of, share] = g[block, share, h].reshape(current.shape[3:])
                 products = []
                 for k in range(slots):
                     column = cols_s[k, block]
                     share, within = column // share_tiles, column % share_tiles
-                    piece = current[seat_of, share, within % packed_tiles]
+                    piece = current[h, seat_of, share, within % packed_tiles]
                     piece = jnp.where(of_lane == within // packed_tiles, piece, jnp.zeros_like(piece))
                     products.append(
                         jnp.dot(tiles_v[block, k], piece, preferred_element_type=jnp.float32)
@@ -601,8 +600,6 @@
     for h in range(chunks - 1):
         take(h)
     core_back(1 - c).wait_recv()
-    sum_copy = local(total, sum_ref, 12)
-    sum_copy.start()
 
     core_copy().wait_send()
     pair_copy().wait_send()
@@ -653,7 +650,6 @@
 
                 send(beyond, share, h, 3, near_core).wait_send()
 
-    sum_copy.wait()
     for h in range(chunks):
         back_copy(h).wait_send()
     take(chunks - 1)
@@ -680,7 +676,7 @@
         in_specs=[pl.BlockSpec(memory_space=pl.ANY)] * 9,
         out_specs=(
             pl.BlockSpec(memory_space=pltpu.VMEM),
-            pl.BlockSpec(memory_space=pl.ANY),
+            pl.BlockSpec(memory_space=pltpu.VMEM),
         ),
         scratch_shapes=[
             pltpu.VMEM(rows.shape, i32),
@@ -696,7 +692,7 @@
             pltpu.VMEM(tiles.shape, bf16),
             pltpu.VMEM((blocks, copies, CHUNKS, chunk_rows, half), bf16),
             pltpu.VMEM((CHUNKS, chunk_rows, half), bf16),
-            pltpu.VMEM((count, copies, chunk_rows // side, side, half), bf16),
+            pltpu.VMEM((CHUNKS, count, copies, chunk_rows // side, side, half), bf16),
             pltpu.VMEM((CHUNKS, count * slots + 1, side, half), f32),
             pltpu.VMEM((2, *rows.shape), i32),
             pltpu.SMEM((2, *rows.shape), i32),
@@ -708,8 +704,7 @@
             pltpu.VMEM((width // 2, width), f32),
             pltpu.VMEM((width // 2, width), f32),
             pltpu.VMEM((seats, width // 2 // owners, width), f32),
-            pltpu.VMEM((2 * width, width), f32),
-            dma((13,)),
+            dma((12,)),
             dma((4, blocks, copies, CHUNKS)),
             dma((blocks, copies, CHUNKS)),
             dma((CHUNKS,)),
@@ -722,8 +717,34 @@
             dma((2, seats)),
             dma((2, seats)),
         ],
-        compiler_params=pltpu.CompilerParams(collective_id=0, has_side_effects=True, vmem_limit_bytes=54 << 20),
+        compiler_params=pltpu.CompilerParams(collective_id=0, has_side_effects=True, vmem_limit_bytes=60 << 20),
     )(*(pltpu.with_memory_space_constraint(operand, pltpu.HBM) for operand in operands))
+
+
+def finish_kernel(grad_ref, sums_ref, *refs):
+    outs, sem = refs[:3], refs[3]
+    width = sums_ref.shape[1]
+    sources = (grad_ref, sums_ref.at[pl.ds(0, width)], sums_ref.at[pl.ds(width, width)])
+    copies = [
+        pltpu.make_async_copy(src, dst, sem.at[n]) for n, (src, dst) in enumerate(zip(sources, outs))
+    ]
+    for copy in copies:
+        copy.start()
+    for copy in copies:
+        copy.wait()
+
+
+def finish(feature_grad, sums):
+    width = sums.shape[1]
+    square = jax.ShapeDtypeStruct((width, width), sums.dtype)
+    return pl.pallas_call(
+        finish_kernel,
+        out_shape=(jax.ShapeDtypeStruct(feature_grad.shape, feature_grad.dtype), square, square),
+        in_specs=[pl.BlockSpec(memory_space=pl.ANY)] * 2,
+        out_specs=(pl.BlockSpec(memory_space=pl.ANY),) * 3,
+        scratch_shapes=[pltpu.SemaphoreType.DMA((3,))],
+        compiler_params=pltpu.CompilerParams(vmem_limit_bytes=1 << 20),
+    )(feature_grad, sums)
 
 
 def by_columns(
@@ -746,7 +767,7 @@
         blocks,
         copies,
     )
-    return (feature_grad, sums[:width], sums[width:])
+    return finish(feature_grad, sums)
 
 
 def on_device(

time: 62.5 us -> 61.9 us (level)
  local copies, waits for them, and re-layouts: 1.8 us -> 0 us
  Pallas kernels: 60 us -> 61.1 us
    pallas_call x0 -> x1, Pallas kernels: none -> 1.16 us  [finish(): pl.pallas_call(finish_kernel, out_shape=(jax.ShapeDtypeStruct(feature_gra...]
    unnamed x1 -> x0, local copies, waits for them, and re-layouts: 0.97 us -> none
    slice x1 -> x0, local copies, waits for them, and re-layouts: 0.82 us -> none  [by_columns(): return (feature_grad, sums[:width], sums[width:])]
where the time goes in v3:
time: 61.9 us; the launch traced here: 61.7 us
  Pallas kernels  61.1 us (99%)
  between operations  0.64 us (1%)
    pallas_call x1, Pallas kernels, layer(): pl.pallas_call(functools.partial(layer_kernel, blocks, copies, scale), ou...  59.9 us

profile of v3, /device:TPU:0, one launch (start us, length us, event | category | flops | bytes accessed | tf_op | source)
XLA Modules:
  0.0 61.7 jit_solution(8715550345880106093)
XLA Ops:
  0.6 59.9 %shard_map.112 = (f32[1024,256]{1,0:T(8,128)S(1)}, f32[512,256]{1,0:T(8,128)S(1)}) custom-call(s32[8,16]{1,0:T(8,128)} %bitcast.8, s32[8,16]{1,0:T(8,128)} %bitcast.9, s32[1,16]{1,0:T(1,128)} %counts_ref.1, bf16[1024,256]{1,0:T(8,128)(2,1)} %features_ref.1, bf16[1024,256]{1,0:T(8,128)(2,1)} %aggregated_ref.1, bf16[1024,256]{1,0:T(8,128)(2,1)} %grad_ref.1, ...), custom_call_target="tpu_custom_call" | custom-call | tf_op jit(solution)/shard_map/pallas_call | solution.py:670
  60.6 1.2 %shard_map.113 = (f32[1024,256]{1,0:T(8,128)}, f32[256,256]{1,0:T(8,128)}, f32[256,256]{1,0:T(8,128)}) custom-call(f32[1024,256]{1,0:T(8,128)S(1)} %get-tuple-element.5.grad_ref, f32[512,256]{1,0:T(8,128)S(1)} %get-tuple-element.6.sums_ref), custom_call_target="tpu_custom_call" | custom-call | tf_op jit(solution)/shard_map/pallas_call | solution.py:740

commit v4 on v3

--- a/solution.py
+++ b/solution.py
@@ -571,9 +571,9 @@
 
     events = [
         (0.1, make_terms),
-        (0.2, chain_links),
-        (0.3, lambda: links_copy().start()),
-        (0.9, over_cores),
+        (1.2, chain_links),
+        (1.25, lambda: links_copy().start()),
+        (1.15, over_cores),
         (1.45, lambda: (links_copy().wait(), loads[10].wait())),
         (1.9, over_pair),
         (2.9, self_part),

time: 61.9 us -> 61.9 us (level)
  no operation moved by 1% of the time
where the time goes in v4:
time: 61.9 us; the launch traced here: 61.7 us
  Pallas kernels  61.1 us (99%)
  between operations  0.64 us (1%)
    pallas_call x1, Pallas kernels, layer(): pl.pallas_call(functools.partial(layer_kernel, blocks, copies, scale), ou...  59.9 us

profile of v4, /device:TPU:0, one launch (start us, length us, event | category | flops | bytes accessed | tf_op | source)
XLA Modules:
  0.0 61.7 jit_solution(4155538819231851605)
XLA Ops:
  0.6 59.9 %shard_map.112 = (f32[1024,256]{1,0:T(8,128)S(1)}, f32[512,256]{1,0:T(8,128)S(1)}) custom-call(s32[8,16]{1,0:T(8,128)} %bitcast.8, s32[8,16]{1,0:T(8,128)} %bitcast.9, s32[1,16]{1,0:T(1,128)} %counts_ref.1, bf16[1024,256]{1,0:T(8,128)(2,1)} %features_ref.1, bf16[1024,256]{1,0:T(8,128)(2,1)} %aggregated_ref.1, bf16[1024,256]{1,0:T(8,128)(2,1)} %grad_ref.1, ...), custom_call_target="tpu_custom_call" | custom-call | tf_op jit(solution)/shard_map/pallas_call | solution.py:670
  60.6 1.2 %shard_map.113 = (f32[1024,256]{1,0:T(8,128)}, f32[256,256]{1,0:T(8,128)}, f32[256,256]{1,0:T(8,128)}) custom-call(f32[1024,256]{1,0:T(8,128)S(1)} %get-tuple-element.5.grad_ref, f32[512,256]{1,0:T(8,128)S(1)} %get-tuple-element.6.sums_ref), custom_call_target="tpu_custom_call" | custom-call | tf_op jit(solution)/shard_map/pallas_call | solution.py:740
